TPU v7x, 512 devices: a whole 4x4x16 slice. The times are simulated.
512 devices in a mesh: seq: 64 (over z, y), dp: 8 (over x, core).
Axes of the slice: x: 4, y: 4, z: 16, core: 2. Of those that a mesh axis runs over, the one named last changes fastest.
Arguments:
- queries: bfloat16 [8, 8192, 2048], P('dp', 'seq'), may hold values from -40 to 40
- keys: bfloat16 [8, 8192, 2048], P('dp', 'seq'), may hold values from -6 to 6
- values: bfloat16 [8, 8192, 2048], P('dp', 'seq'), may hold values from -6 to 6
- grad_out: bfloat16 [8, 8192, 2048], P('dp', 'seq'), may hold values from -48 to 48
- lengths: int32 [8], P('dp'), may hold values from 1024 to 8192, as said below
- fields: int32 [8, 8192], P('dp', 'seq'), may hold values from 0 to 63
- field_bias: bfloat16 [16, 64], replicated, may hold values from -6 to 6
Outputs:
- grad_queries: bfloat16 [8, 8192, 2048], P('dp', 'seq')
- grad_keys: bfloat16 [8, 8192, 2048], P('dp', 'seq')
- grad_values: bfloat16 [8, 8192, 2048], P('dp', 'seq')
- grad_bias: float32 [16, 64], replicated
Inputs may be any that keep to these rules, and one draw needn't show every extreme that they name: `lengths`: the valid positions of a sequence form a prefix; in every draw some sequence is full.
All inputs are finite; a program needn't handle non-finite values.
Results may differ from a plain program's by a relative error of at most 0.0077.
Values may be sent and summed in bfloat16 or wider, within the bound.
A program may use at most 128 MiB of HBM per device.

v0:
```python
import jax
import jax.numpy as jnp
from jax import lax
from jax.sharding import PartitionSpec as P

HEADS = 16
HEAD_DIM = 128
WINDOW = 512
FIELDS = 64


def passed_along(value, axis, steps):
    count = lax.axis_size(axis)
    first, last = (max(0, -steps), min(count, count - steps))
    return lax.ppermute(value, axis, [(source, source + steps) for source in range(first, last)])


def split_heads(rows):
    return rows.reshape(rows.shape[0], HEADS, HEAD_DIM)


def band_mask(query_places, key_places, length):
    not_after = key_places[None, :] <= query_places[:, None]
    inside = key_places[None, :] > query_places[:, None] - WINDOW
    started = key_places[None, :] >= 0
    live_rows = query_places[:, None] < length
    return not_after & inside & started & live_rows


def logits_of(query_heads, key_heads, key_bias):
    factor = HEAD_DIM ** (-0.5)
    products = jnp.einsum(
        "qhd,khd->hqk", query_heads, key_heads, preferred_element_type=jnp.float32
    )
    return products * factor + key_bias[:, None, :]


def grad_logits_of(attn_weights, row_delta, grad_heads, value_heads):
    grad_probs = jnp.einsum(
        "qhd,khd->hqk", grad_heads, value_heads, preferred_element_type=jnp.float32
    )
    return attn_weights * (grad_probs - row_delta[:, :, None])


def shards(queries, keys, values, grad_out, lengths, fields, field_bias):
    tok_rows = queries.shape[1]
    row_width = queries.shape[2]
    length = lengths[0]
    query_own = queries[0]
    key_own = keys[0]
    value_own = values[0]
    grad_own = grad_out[0]
    reach_blocks = WINDOW // tok_rows
    factor = HEAD_DIM ** (-0.5)
    block_index = lax.axis_index("seq")
    onehot = (fields[0][:, None] == jnp.arange(FIELDS, dtype=jnp.int32)[None, :]).astype(
        jnp.bfloat16
    )
    own_bias = jnp.dot(field_bias, onehot.T, preferred_element_type=jnp.float32).astype(
        jnp.bfloat16
    )
    package = (key_own, value_own, own_bias)
    arrived = []
    for distance in range(1, reach_blocks + 1):
        arrived.append(passed_along((package[0], package[1], package[2]), "seq", distance))
    ordered = arrived[::-1] + [package]
    key_all = jnp.concatenate([arrival[0] for arrival in ordered], axis=0)
    value_all = jnp.concatenate([arrival[1] for arrival in ordered], axis=0)
    bias_all = jnp.concatenate([arrival[2] for arrival in ordered], axis=1).astype(jnp.float32)
    query_places = block_index * tok_rows + jnp.arange(tok_rows, dtype=jnp.int32)
    key_places = (block_index - reach_blocks) * tok_rows + jnp.arange(
        (reach_blocks + 1) * tok_rows, dtype=jnp.int32
    )
    query_heads = split_heads(query_own)
    grad_heads = split_heads(grad_own)
    key_heads = split_heads(key_all)
    value_heads = split_heads(value_all)
    logits = logits_of(query_heads, key_heads, bias_all)
    visible = band_mask(query_places, key_places, length)[None]
    live_rows = (query_places < length)[None, :, None]
    row_peak = jnp.max(jnp.where(visible, logits, -1e30), axis=2, keepdims=True)
    powers = jnp.where(visible, jnp.exp(logits - row_peak), 0.0)
    totals = jnp.where(live_rows, jnp.sum(powers, axis=2, keepdims=True), 1.0)
    attn_weights = powers / totals
    weights_low = attn_weights.astype(jnp.bfloat16)
    outputs = jnp.einsum(
        "hqk,khd->qhd", weights_low, value_heads, preferred_element_type=jnp.float32
    )
    row_delta = jnp.einsum("qhd,qhd->hq", grad_heads.astype(jnp.float32), outputs)
    grad_logits = grad_logits_of(attn_weights, row_delta, grad_heads, value_heads)
    grad_low = grad_logits.astype(jnp.bfloat16)
    grad_query = (
        jnp.einsum("hqk,khd->qhd", grad_low, key_heads, preferred_element_type=jnp.float32) * factor
    )
    own_cols = reach_blocks * tok_rows
    grad_key = (
        jnp.einsum(
            "hqk,qhd->khd", grad_low, query_heads, preferred_element_type=jnp.float32
        ).reshape(-1, row_width)
        * factor
    )
    grad_value = jnp.einsum(
        "hqk,qhd->khd", weights_low, grad_heads, preferred_element_type=jnp.float32
    ).reshape(-1, row_width)
    column = jnp.sum(grad_logits, axis=1)
    key_total = grad_key[own_cols:]
    value_total = grad_value[own_cols:]
    column_total = column[:, own_cols:]
    for distance in range(1, reach_blocks + 1):
        first_row = (reach_blocks - distance) * tok_rows
        returned = passed_along(
            (
                grad_key[first_row : first_row + tok_rows],
                grad_value[first_row : first_row + tok_rows],
                column[:, first_row : first_row + tok_rows],
            ),
            "seq",
            -distance,
        )
        key_total = key_total + returned[0]
        value_total = value_total + returned[1]
        column_total = column_total + returned[2]
    bias_local = jnp.dot(column_total, onehot.astype(jnp.float32), precision=lax.Precision.HIGHEST)
    query_low = grad_query.reshape(tok_rows, row_width).astype(jnp.bfloat16)
    key_low = key_total.astype(jnp.bfloat16)
    value_low = value_total.astype(jnp.bfloat16)
    bias_total = lax.psum(bias_local, ("seq", "dp"))
    return (
        query_low.reshape(1, tok_rows, row_width),
        key_low.reshape(1, tok_rows, row_width),
        value_low.reshape(1, tok_rows, row_width),
        bias_total,
    )


def solution(mesh):
    return jax.shard_map(
        shards,
        mesh=mesh,
        in_specs=(
            P("dp", "seq", None),
            P("dp", "seq", None),
            P("dp", "seq", None),
            P("dp", "seq", None),
            P("dp"),
            P("dp", "seq"),
            P(),
        ),
        out_specs=(P("dp", "seq", None), P("dp", "seq", None), P("dp", "seq", None), P()),
        check_vma=False,
    )
```

profile of v0, /device:TPU:1, one launch (start us, length us, event | category | flops | bytes accessed | tf_op | source)
XLA Modules:
  0.0 491.5 jit_solution(1476968906301964713)
XLA Ops:
  2.2 4.2 collective-permute-start.7
  6.4 4.5 collective-permute-start.6
  12.2 2.6 collective-permute-start.11
  14.9 4.8 collective-permute-start.10
  19.7 4.2 collective-permute-start.9
  24.6 2.6 collective-permute-start.5
  27.3 4.8 collective-permute-start.4
  38.1 5.2 %collective-permute-done.5 = bf16[16,128]{1,0:T(8,128)(2,1)S(1)} collective-permute-done((bf16[16,128]{1,0:T(8,128)(2,1)S(1)}, bf16[16,128]{1,0:T(8,128)(2,1)S(1)}, u32[]{:S(2)}, u32[]{:S(2)}) %collective-permute-start.5) | collective-permute-done | bytes 4128 | tf_op jit(solution)/shard_map/ppermute | solution.py:15
  44.7 18.3 %collective-permute-start.3 = (bf16[128,2048]{0,1:T(8,128)(2,1)S(1)}, bf16[128,2048]{0,1:T(8,128)(2,1)}, u32[]{:S(2)}, u32[]{:S(2)}) collective-permute-start(bf16[128,2048]{0,1:T(8,128)(2,1)S(1)} %bitcast.102), channel_id=1, source_target_pairs={{0,8},{8,16},{16,24},{24,32},{32,40},{40,48},{48,56},{56,64},{64,7... | collective-permute-start | bytes 1572872 | tf_op jit(solution)/shard_map/ppermute | solution.py:15
  63.0 9.7 %collective-permute-start.2 = (bf16[128,2048]{0,1:T(8,128)(2,1)S(1)}, bf16[128,2048]{0,1:T(8,128)(2,1)}, u32[]{:S(2)}, u32[]{:S(2)}) collective-permute-start(bf16[128,2048]{0,1:T(8,128)(2,1)S(1)} %bitcast.103), channel_id=1, source_target_pairs={{0,16},{8,24},{16,32},{24,40},{32,48},{40,56},{48,64},{56,72},{64,... | collective-permute-start | bytes 1572872 | tf_op jit(solution)/shard_map/ppermute | solution.py:15
  72.7 5.3 %collective-permute-start.1 = (bf16[128,2048]{0,1:T(8,128)(2,1)S(1)}, bf16[128,2048]{0,1:T(8,128)(2,1)}, u32[]{:S(2)}, u32[]{:S(2)}) collective-permute-start(bf16[128,2048]{0,1:T(8,128)(2,1)S(1)} %bitcast.104), channel_id=1, source_target_pairs={{0,24},{8,32},{16,40},{24,48},{32,56},{40,64},{48,72},{56,80},{64,... | collective-permute-start | bytes 1572872 | tf_op jit(solution)/shard_map/ppermute | solution.py:15
  89.5 4.0 collective-permute-done.1
  104.6 7.6 %fusion.34 = (f32[16,128]{1,0:T(8,128)S(1)}, f32[16,128,640]{1,2,0:T(8,128)}) fusion(f32[16,640]{1,0:T(8,128)S(1)} %convert_element_type.46, pred[128,640]{0,1:T(8,128)(4,1)S(1)} %and_and_fusion, bf16[640,16,128]{2,0,1:T(8,128)(2,1)} %constant_dynamic-update-slice_fusion, bf16[128,16,128]{0,2,1:T(8,128)(2,1)} %bitcast.94), kind=kOutput, calls=%fused_computation.67 | convolution fusion | flops 681575040 | bytes 8519680 | tf_op jit(solution)/shard_map/sub | solution.py:82
  117.3 3.3 fusion.8
  122.6 2.6 copy.69
  126.9 5.2 %fusion.35 = (f32[16,640]{1,0:T(8,128)S(1)}, bf16[16,128,640]{1,2,0:T(8,128)(2,1)S(1)}) fusion(f32[16,128]{1,0:T(8,128)S(1)} %copy.70, bf16[640,16,128]{2,0,1:T(8,128)(2,1)} %copy-done.5, bf16[128,16,128]{0,2,1:T(8,128)(2,1)} %copy.55, f32[16,128,640]{1,2,0:T(8,128)} %get-tuple-element.27, f32[16,128]{1,0:T(8,128)S(1)} %broadcast_select_fusion), kind=kOutput, calls=%fused_computation.68 | convolution fusion | flops 342087680 | bytes 11067392 | tf_op jit(solution)/shard_map/qhd,khd->hqk/dot_general | solution.py:39
  141.0 2.6 copy.50
  152.6 15.2 %collective-permute-done.20 = f32[16,128]{1,0:T(8,128)S(1)} collective-permute-done((f32[16,128]{1,0:T(8,128)S(1)}, f32[16,128]{1,0:T(8,128)S(1)}, u32[]{:S(2)}, u32[]{:S(2)}) %collective-permute-start.20) | collective-permute-done | bytes 8224 | tf_op jit(solution)/shard_map/ppermute | solution.py:15
  169.2 109.7 %collective-permute-done.23 = f32[16,128]{1,0:T(8,128)S(1)} collective-permute-done((f32[16,128]{1,0:T(8,128)S(1)}, f32[16,128]{1,0:T(8,128)S(1)}, u32[]{:S(2)}, u32[]{:S(2)}) %collective-permute-start.23) | collective-permute-done | bytes 8224 | tf_op jit(solution)/shard_map/ppermute | solution.py:15
  281.2 2.8 collective-permute-done.22
  290.2 2.7 copy.59
  300.7 2.8 fusion.11
  306.6 178.1 %psum.7 = f32[16,64]{1,0:T(8,128)} all-reduce(f32[16,64]{1,0:T(8,128)S(1)} %fusion.22), channel_id=1, replica_groups=mesh['seq'=64,'dp'=8] {'seq','dp'}, use_global_device_ids=true, to_apply=%region_3.4 | all-reduce | flops 1024 | bytes 8192 | tf_op jit(solution)/shard_map/psum | solution.py:127
  488.1 3.4 fusion.19
  (121 shorter events, 83.4 us)
Async XLA Ops:
  2.2 22.4 %collective-permute-start.7 = (bf16[16,128]{1,0:T(8,128)(2,1)S(1)}, bf16[16,128]{1,0:T(8,128)(2,1)S(1)}, u32[]{:S(2)}, u32[]{:S(2)}) collective-permute-start(bf16[16,128]{1,0:T(8,128)(2,1)S(1)} %fusion.14), channel_id=1, source_target_pairs={{0,8},{8,16},{16,24},{24,32},{32,40},{40,48},{48,56},{56,64},{64,7... | collective-permute-start | bytes 12296 | tf_op jit(solution)/shard_map/ppermute | solution.py:15
  6.4 20.9 %collective-permute-start.6 = (bf16[16,128]{1,0:T(8,128)(2,1)S(1)}, bf16[16,128]{1,0:T(8,128)(2,1)S(1)}, u32[]{:S(2)}, u32[]{:S(2)}) collective-permute-start(bf16[16,128]{1,0:T(8,128)(2,1)S(1)} %fusion.14), channel_id=1, source_target_pairs={{0,16},{8,24},{16,32},{24,40},{32,48},{40,56},{48,64},{56,72},{64,... | collective-permute-start | bytes 12296 | tf_op jit(solution)/shard_map/ppermute | solution.py:15
  12.2 50.8 %collective-permute-start.11 = (bf16[128,2048]{0,1:T(8,128)(2,1)S(1)}, bf16[128,2048]{0,1:T(8,128)(2,1)S(1)}, u32[]{:S(2)}, u32[]{:S(2)}) collective-permute-start(bf16[128,2048]{0,1:T(8,128)(2,1)S(1)} %bitcast.96), channel_id=1, source_target_pairs={{0,8},{8,16},{16,24},{24,32},{32,40},{40,48},{48,56},{56,64},{64,7... | collective-permute-start | bytes 1572872 | tf_op jit(solution)/shard_map/ppermute | solution.py:15
  14.9 57.8 %collective-permute-start.10 = (bf16[128,2048]{0,1:T(8,128)(2,1)S(1)}, bf16[128,2048]{0,1:T(8,128)(2,1)S(1)}, u32[]{:S(2)}, u32[]{:S(2)}) collective-permute-start(bf16[128,2048]{0,1:T(8,128)(2,1)S(1)} %bitcast.97), channel_id=1, source_target_pairs={{0,16},{8,24},{16,32},{24,40},{32,48},{40,56},{48,64},{56,72},{64,... | collective-permute-start | bytes 1572872 | tf_op jit(solution)/shard_map/ppermute | solution.py:15
  19.7 58.3 %collective-permute-start.9 = (bf16[128,2048]{0,1:T(8,128)(2,1)S(1)}, bf16[128,2048]{0,1:T(8,128)(2,1)}, u32[]{:S(2)}, u32[]{:S(2)}) collective-permute-start(bf16[128,2048]{0,1:T(8,128)(2,1)S(1)} %bitcast.98), channel_id=1, source_target_pairs={{0,24},{8,32},{16,40},{24,48},{32,56},{40,64},{48,72},{56,80},{64,... | collective-permute-start | bytes 1572872 | tf_op jit(solution)/shard_map/ppermute | solution.py:15
  24.6 18.7 %collective-permute-start.5 = (bf16[16,128]{1,0:T(8,128)(2,1)S(1)}, bf16[16,128]{1,0:T(8,128)(2,1)S(1)}, u32[]{:S(2)}, u32[]{:S(2)}) collective-permute-start(bf16[16,128]{1,0:T(8,128)(2,1)S(1)} %fusion.14), channel_id=1, source_target_pairs={{0,24},{8,32},{16,40},{24,48},{32,56},{40,64},{48,72},{56,80},{64,... | collective-permute-start | bytes 12296 | tf_op jit(solution)/shard_map/ppermute | solution.py:15
  27.3 17.4 %collective-permute-start.4 = (bf16[16,128]{1,0:T(8,128)(2,1)S(1)}, bf16[16,128]{1,0:T(8,128)(2,1)S(1)}, u32[]{:S(2)}, u32[]{:S(2)}) collective-permute-start(bf16[16,128]{1,0:T(8,128)(2,1)S(1)} %fusion.14), channel_id=1, source_target_pairs={{0,32},{8,40},{16,48},{24,56},{32,64},{40,72},{48,80},{56,88},{64,... | collective-permute-start | bytes 12296 | tf_op jit(solution)/shard_map/ppermute | solution.py:15
  43.3 41.0 %collective-permute-start.8 = (bf16[128,2048]{0,1:T(8,128)(2,1)S(1)}, bf16[128,2048]{0,1:T(8,128)(2,1)S(1)}, u32[]{:S(2)}, u32[]{:S(2)}) collective-permute-start(bf16[128,2048]{0,1:T(8,128)(2,1)S(1)} %bitcast.100), channel_id=1, source_target_pairs={{0,32},{8,40},{16,48},{24,56},{32,64},{40,72},{48,80},{56,88},{64,... | collective-permute-start | bytes 1572872 | tf_op jit(solution)/shard_map/ppermute | solution.py:15
  44.7 40.7 %collective-permute-start.3 = (bf16[128,2048]{0,1:T(8,128)(2,1)S(1)}, bf16[128,2048]{0,1:T(8,128)(2,1)}, u32[]{:S(2)}, u32[]{:S(2)}) collective-permute-start(bf16[128,2048]{0,1:T(8,128)(2,1)S(1)} %bitcast.102), channel_id=1, source_target_pairs={{0,8},{8,16},{16,24},{24,32},{32,40},{40,48},{48,56},{56,64},{64,7... | collective-permute-start | bytes 1572872 | tf_op jit(solution)/shard_map/ppermute | solution.py:15
  63.0 24.4 %collective-permute-start.2 = (bf16[128,2048]{0,1:T(8,128)(2,1)S(1)}, bf16[128,2048]{0,1:T(8,128)(2,1)}, u32[]{:S(2)}, u32[]{:S(2)}) collective-permute-start(bf16[128,2048]{0,1:T(8,128)(2,1)S(1)} %bitcast.103), channel_id=1, source_target_pairs={{0,16},{8,24},{16,32},{24,40},{32,48},{40,56},{48,64},{56,72},{64,... | collective-permute-start | bytes 1572872 | tf_op jit(solution)/shard_map/ppermute | solution.py:15
  72.7 20.8 %collective-permute-start.1 = (bf16[128,2048]{0,1:T(8,128)(2,1)S(1)}, bf16[128,2048]{0,1:T(8,128)(2,1)}, u32[]{:S(2)}, u32[]{:S(2)}) collective-permute-start(bf16[128,2048]{0,1:T(8,128)(2,1)S(1)} %bitcast.104), channel_id=1, source_target_pairs={{0,24},{8,32},{16,40},{24,48},{32,56},{40,64},{48,72},{56,80},{64,... | collective-permute-start | bytes 1572872 | tf_op jit(solution)/shard_map/ppermute | solution.py:15
  78.0 17.5 %collective-permute-start = (bf16[128,2048]{0,1:T(8,128)(2,1)S(1)}, bf16[128,2048]{0,1:T(8,128)(2,1)}, u32[]{:S(2)}, u32[]{:S(2)}) collective-permute-start(bf16[128,2048]{0,1:T(8,128)(2,1)S(1)} %bitcast.105), channel_id=1, source_target_pairs={{0,32},{8,40},{16,48},{24,56},{32,64},{40,72},{48,80},{56,88},{64,... | collective-permute-start | bytes 1572872 | tf_op jit(solution)/shard_map/ppermute | solution.py:15
  143.6 153.2 %collective-permute-start.12 = (f32[128,2048]{0,1:T(8,128)}, f32[128,2048]{0,1:T(8,128)}, u32[]{:S(2)}, u32[]{:S(2)}) collective-permute-start(f32[128,2048]{0,1:T(8,128)} %bitcast.111), channel_id=1, source_target_pairs={{8,0},{16,8},{24,16},{32,24},{40,32},{48,40},{56,48},{64,56},{72,6... | collective-permute-start | bytes 3145736 | tf_op jit(solution)/shard_map/ppermute | solution.py:15
  144.8 153.2 %collective-permute-start.13 = (f32[128,2048]{0,1:T(8,128)}, f32[128,2048]{0,1:T(8,128)}, u32[]{:S(2)}, u32[]{:S(2)}) collective-permute-start(f32[128,2048]{0,1:T(8,128)} %bitcast.110), channel_id=1, source_target_pairs={{16,0},{24,8},{32,16},{40,24},{48,32},{56,40},{64,48},{72,56},{80,... | collective-permute-start | bytes 3145736 | tf_op jit(solution)/shard_map/ppermute | solution.py:15
  146.1 153.2 %collective-permute-start.14 = (f32[128,2048]{0,1:T(8,128)}, f32[128,2048]{0,1:T(8,128)}, u32[]{:S(2)}, u32[]{:S(2)}) collective-permute-start(f32[128,2048]{0,1:T(8,128)} %bitcast.108), channel_id=1, source_target_pairs={{24,0},{32,8},{40,16},{48,24},{56,32},{64,40},{72,48},{80,56},{88,... | collective-permute-start | bytes 3145736 | tf_op jit(solution)/shard_map/ppermute | solution.py:15
  147.5 20.4 %collective-permute-start.20 = (f32[16,128]{1,0:T(8,128)S(1)}, f32[16,128]{1,0:T(8,128)S(1)}, u32[]{:S(2)}, u32[]{:S(2)}) collective-permute-start(f32[16,128]{1,0:T(8,128)S(1)} %get-tuple-element.22), channel_id=1, source_target_pairs={{8,0},{16,8},{24,16},{32,24},{40,32},{48,40},{56,48},{64,56},{72,6... | collective-permute-start | bytes 24584 | tf_op jit(solution)/shard_map/ppermute | solution.py:15
  148.8 130.1 %collective-permute-start.23 = (f32[16,128]{1,0:T(8,128)S(1)}, f32[16,128]{1,0:T(8,128)S(1)}, u32[]{:S(2)}, u32[]{:S(2)}) collective-permute-start(f32[16,128]{1,0:T(8,128)S(1)} %get-tuple-element.23), channel_id=1, source_target_pairs={{32,0},{40,8},{48,16},{56,24},{64,32},{72,40},{80,48},{88,56},{96,... | collective-permute-start | bytes 24584 | tf_op jit(solution)/shard_map/ppermute | solution.py:15
  167.9 116.2 %collective-permute-start.22 = (f32[16,128]{1,0:T(8,128)S(1)}, f32[16,128]{1,0:T(8,128)S(1)}, u32[]{:S(2)}, u32[]{:S(2)}) collective-permute-start(f32[16,128]{1,0:T(8,128)S(1)} %get-tuple-element.24), channel_id=1, source_target_pairs={{24,0},{32,8},{40,16},{48,24},{56,32},{64,40},{72,48},{80,56},{88,... | collective-permute-start | bytes 24584 | tf_op jit(solution)/shard_map/ppermute | solution.py:15
  278.9 205.8 %collective-permute-start.15 = (f32[128,2048]{0,1:T(8,128)}, f32[128,2048]{0,1:T(8,128)}, u32[]{:S(2)}, u32[]{:S(2)}) collective-permute-start(f32[128,2048]{0,1:T(8,128)} %bitcast.109), channel_id=1, source_target_pairs={{32,0},{40,8},{48,16},{56,24},{64,32},{72,40},{80,48},{88,56},{96,... | collective-permute-start | bytes 3145736 | tf_op jit(solution)/shard_map/ppermute | solution.py:15
  284.0 11.4 %collective-permute-start.21 = (f32[16,128]{1,0:T(8,128)S(1)}, f32[16,128]{1,0:T(8,128)S(1)}, u32[]{:S(2)}, u32[]{:S(2)}) collective-permute-start(f32[16,128]{1,0:T(8,128)S(1)} %get-tuple-element.25), channel_id=1, source_target_pairs={{16,0},{24,8},{32,16},{40,24},{48,32},{56,40},{64,48},{72,56},{80,... | collective-permute-start | bytes 24584 | tf_op jit(solution)/shard_map/ppermute | solution.py:15
  295.5 192.7 %collective-permute-start.17 = (f32[128,2048]{1,0:T(8,128)}, f32[128,2048]{1,0:T(8,128)}, u32[]{:S(2)}, u32[]{:S(2)}) collective-permute-start(f32[128,2048]{1,0:T(8,128)} %copy.58), channel_id=1, source_target_pairs={{16,0},{24,8},{32,16},{40,24},{48,32},{56,40},{64,48},{72,56},{80,... | collective-permute-start | bytes 3145736 | tf_op jit(solution)/shard_map/ppermute | solution.py:15
  296.8 191.4 %collective-permute-start.18 = (f32[128,2048]{1,0:T(8,128)}, f32[128,2048]{1,0:T(8,128)}, u32[]{:S(2)}, u32[]{:S(2)}) collective-permute-start(f32[128,2048]{1,0:T(8,128)} %copy.59), channel_id=1, source_target_pairs={{24,0},{32,8},{40,16},{48,24},{56,32},{64,40},{72,48},{80,56},{88,... | collective-permute-start | bytes 3145736 | tf_op jit(solution)/shard_map/ppermute | solution.py:15
  298.1 190.1 %collective-permute-start.19 = (f32[128,2048]{1,0:T(8,128)}, f32[128,2048]{1,0:T(8,128)}, u32[]{:S(2)}, u32[]{:S(2)}) collective-permute-start(f32[128,2048]{1,0:T(8,128)} %copy.60), channel_id=1, source_target_pairs={{32,0},{40,8},{48,16},{56,24},{64,32},{72,40},{80,48},{88,56},{96,... | collective-permute-start | bytes 3145736 | tf_op jit(solution)/shard_map/ppermute | solution.py:15
  299.4 188.7 %collective-permute-start.16 = (f32[128,2048]{1,0:T(8,128)}, f32[128,2048]{1,0:T(8,128)}, u32[]{:S(2)}, u32[]{:S(2)}) collective-permute-start(f32[128,2048]{1,0:T(8,128)} %copy.56), channel_id=1, source_target_pairs={{8,0},{16,8},{24,16},{32,24},{40,32},{48,40},{56,48},{64,56},{72,6... | collective-permute-start | bytes 3145736 | tf_op jit(solution)/shard_map/ppermute | solution.py:15
  (15 other events, 257.7 us)
where the time goes:
time: 493 us; the launch traced here: 492 us
  blocking collectives  178 us (36%)
  waiting for transfers between devices  137 us (28%)
  starting transfers between devices  80.2 us (16%)
  local copies, waits for them, and re-layouts  63.1 us (13%)
  matrix products  20.4 us (4%)
  other arithmetic  10.9 us (2%)
    psum x1, blocking collectives, shards(): bias_total = lax.psum(bias_local, ('seq', 'dp'))  178 us
    ppermute x24, waiting for transfers between devices, passed_along(): lax.ppermute(value, axis, [(source, source + steps) for source in range(f...  137 us
    ppermute x24, starting transfers between devices, passed_along(): lax.ppermute(value, axis, [(source, source + steps) for source in range(f...  80.2 us
    unnamed x48, local copies, waits for them, and re-layouts  20.6 us
    slice x4, local copies, waits for them, and re-layouts, shards(): grad_key[first_row:first_row + tok_rows]  10.2 us
    slice x5, local copies, waits for them, and re-layouts, shards(): grad_value[first_row:first_row + tok_rows]  9.92 us
  transfers between devices with their start and end apart: 24, of which 5 were waited for; matrix products, arithmetic and copies ran while one was open for 8% of the time, Pallas kernels for 0%

commit v1 on v0

--- a/solution.py
+++ b/solution.py
@@ -124,7 +124,7 @@
     query_low = grad_query.reshape(tok_rows, row_width).astype(jnp.bfloat16)
     key_low = key_total.astype(jnp.bfloat16)
     value_low = value_total.astype(jnp.bfloat16)
-    bias_total = lax.psum(bias_local, ("seq", "dp"))
+    bias_total = lax.psum(lax.psum(bias_local, "dp"), "seq")
     return (
         query_low.reshape(1, tok_rows, row_width),
         key_low.reshape(1, tok_rows, row_width),

time: 493 us -> 554 us (1.12)
  the two profiles are of different devices: /device:TPU:1 before, /device:TPU:134 now
where the time goes in v1:
time: 554 us; the launch traced here: 552 us
  blocking collectives  221 us (40%)
  starting transfers between devices  133 us (24%)
  waiting for transfers between devices  102 us (18%)
  local copies, waits for them, and re-layouts  62.8 us (11%)
  matrix products  20.4 us (4%)
  other arithmetic  10.9 us (2%)
    psum x2, blocking collectives, shards(): bias_total = lax.psum(lax.psum(bias_local, 'dp'), 'seq')  221 us
    ppermute x24, starting transfers between devices, passed_along(): lax.ppermute(value, axis, [(source, source + steps) for source in range(f...  133 us
    ppermute x24, waiting for transfers between devices, passed_along(): lax.ppermute(value, axis, [(source, source + steps) for source in range(f...  102 us
    unnamed x48, local copies, waits for them, and re-layouts  20.5 us
  transfers between devices with their start and end apart: 24, of which 5 were waited for; matrix products, arithmetic and copies ran while one was open for 8% of the time, Pallas kernels for 0%

profile of v1, /device:TPU:134, one launch (start us, length us, event | category | flops | bytes accessed | tf_op | source)
XLA Modules:
  0.0 552.4 jit_solution(16666128271713115883)
XLA Ops:
  2.2 3.6 collective-permute-start.7
  5.8 4.8 collective-permute-start.6
  14.8 5.1 collective-permute-start.10
  20.0 3.7 collective-permute-start.9
  24.4 3.7 collective-permute-start.5
  28.1 5.0 collective-permute-start.4
  39.2 2.9 collective-permute-start.8
  42.2 21.8 %collective-permute-start.3 = (bf16[128,2048]{0,1:T(8,128)(2,1)S(1)}, bf16[128,2048]{0,1:T(8,128)(2,1)}, u32[]{:S(2)}, u32[]{:S(2)}) collective-permute-start(bf16[128,2048]{0,1:T(8,128)(2,1)S(1)} %bitcast.102), channel_id=1, source_target_pairs={{0,8},{8,16},{16,24},{24,32},{32,40},{40,48},{48,56},{56,64},{64,7... | collective-permute-start | bytes 1572872 | tf_op jit(solution)/shard_map/ppermute | solution.py:15
  64.0 9.1 %collective-permute-start.2 = (bf16[128,2048]{0,1:T(8,128)(2,1)S(1)}, bf16[128,2048]{0,1:T(8,128)(2,1)}, u32[]{:S(2)}, u32[]{:S(2)}) collective-permute-start(bf16[128,2048]{0,1:T(8,128)(2,1)S(1)} %bitcast.103), channel_id=1, source_target_pairs={{0,16},{8,24},{16,32},{24,40},{32,48},{40,56},{48,64},{56,72},{64,... | collective-permute-start | bytes 1572872 | tf_op jit(solution)/shard_map/ppermute | solution.py:15
  73.1 5.9 %collective-permute-start.1 = (bf16[128,2048]{0,1:T(8,128)(2,1)S(1)}, bf16[128,2048]{0,1:T(8,128)(2,1)}, u32[]{:S(2)}, u32[]{:S(2)}) collective-permute-start(bf16[128,2048]{0,1:T(8,128)(2,1)S(1)} %bitcast.104), channel_id=1, source_target_pairs={{0,24},{8,32},{16,40},{24,48},{32,56},{40,64},{48,72},{56,80},{64,... | collective-permute-start | bytes 1572872 | tf_op jit(solution)/shard_map/ppermute | solution.py:15
  86.4 11.5 %collective-permute-done.3 = bf16[128,2048]{0,1:T(8,128)(2,1)} collective-permute-done((bf16[128,2048]{0,1:T(8,128)(2,1)S(1)}, bf16[128,2048]{0,1:T(8,128)(2,1)}, u32[]{:S(2)}, u32[]{:S(2)}) %collective-permute-start.3) | collective-permute-done | bytes 524320 | tf_op jit(solution)/shard_map/ppermute | solution.py:15
  113.1 7.6 %fusion.34 = (f32[16,128]{1,0:T(8,128)S(1)}, f32[16,128,640]{1,2,0:T(8,128)}) fusion(f32[16,640]{1,0:T(8,128)S(1)} %convert_element_type.46, pred[128,640]{0,1:T(8,128)(4,1)S(1)} %and_and_fusion, bf16[640,16,128]{2,0,1:T(8,128)(2,1)} %constant_dynamic-update-slice_fusion, bf16[128,16,128]{0,2,1:T(8,128)(2,1)} %bitcast.94), kind=kOutput, calls=%fused_computation.67 | convolution fusion | flops 681575040 | bytes 8519680 | tf_op jit(solution)/shard_map/sub | solution.py:82
  125.8 3.3 fusion.8
  135.3 5.2 fusion.35
  151.9 30.0 %collective-permute-start.12 = (f32[128,2048]{0,1:T(8,128)}, f32[128,2048]{0,1:T(8,128)}, u32[]{:S(2)}, u32[]{:S(2)}) collective-permute-start(f32[128,2048]{0,1:T(8,128)} %bitcast.111), channel_id=1, source_target_pairs={{8,0},{16,8},{24,16},{32,24},{40,32},{48,40},{56,48},{64,56},{72,6... | collective-permute-start | bytes 3145736 | tf_op jit(solution)/shard_map/ppermute | solution.py:15
  188.6 4.0 collective-permute-start.23
  195.2 80.6 %collective-permute-done.20 = f32[16,128]{1,0:T(8,128)S(1)} collective-permute-done((f32[16,128]{1,0:T(8,128)S(1)}, f32[16,128]{1,0:T(8,128)S(1)}, u32[]{:S(2)}, u32[]{:S(2)}) %collective-permute-start.20) | collective-permute-done | bytes 8224 | tf_op jit(solution)/shard_map/ppermute | solution.py:15
  277.7 4.9 collective-permute-done.23
  285.6 3.1 collective-permute-done.22
  288.8 3.5 collective-permute-start.21
  304.1 8.0 %collective-permute-start.17 = (f32[128,2048]{1,0:T(8,128)}, f32[128,2048]{1,0:T(8,128)}, u32[]{:S(2)}, u32[]{:S(2)}) collective-permute-start(f32[128,2048]{1,0:T(8,128)} %copy.58), channel_id=1, source_target_pairs={{16,0},{24,8},{32,16},{40,24},{48,32},{56,40},{64,48},{72,56},{80,... | collective-permute-start | bytes 3145736 | tf_op jit(solution)/shard_map/ppermute | solution.py:15
  324.7 11.1 %psum.14 = f32[16,64]{1,0:T(8,128)S(1)} all-reduce(f32[16,64]{1,0:T(8,128)S(1)} %fusion.22), channel_id=1, replica_groups=mesh['seq'=64,'dp'=8] {'dp'}, use_global_device_ids=true, to_apply=%region_3.4 | all-reduce | flops 1024 | bytes 8192 | tf_op jit(solution)/shard_map/psum | solution.py:127
  335.8 209.7 %psum.15 = f32[16,64]{1,0:T(8,128)} all-reduce(f32[16,64]{1,0:T(8,128)S(1)} %psum.14), channel_id=1, replica_groups=mesh['seq'=64,'dp'=8] {'seq'}, use_global_device_ids=true, to_apply=%region_4.5 | all-reduce | flops 1024 | bytes 8192 | tf_op jit(solution)/shard_map/psum | solution.py:127
  549.0 3.4 fusion.19
  (122 shorter events, 98.8 us)
Async XLA Ops:
  2.2 22.2 %collective-permute-start.7 = (bf16[16,128]{1,0:T(8,128)(2,1)S(1)}, bf16[16,128]{1,0:T(8,128)(2,1)S(1)}, u32[]{:S(2)}, u32[]{:S(2)}) collective-permute-start(bf16[16,128]{1,0:T(8,128)(2,1)S(1)} %fusion.14), channel_id=1, source_target_pairs={{0,8},{8,16},{16,24},{24,32},{32,40},{40,48},{48,56},{56,64},{64,7... | collective-permute-start | bytes 12296 | tf_op jit(solution)/shard_map/ppermute | solution.py:15
  5.8 22.3 %collective-permute-start.6 = (bf16[16,128]{1,0:T(8,128)(2,1)S(1)}, bf16[16,128]{1,0:T(8,128)(2,1)S(1)}, u32[]{:S(2)}, u32[]{:S(2)}) collective-permute-start(bf16[16,128]{1,0:T(8,128)(2,1)S(1)} %fusion.14), channel_id=1, source_target_pairs={{0,16},{8,24},{16,32},{24,40},{32,48},{40,56},{48,64},{56,72},{64,... | collective-permute-start | bytes 12296 | tf_op jit(solution)/shard_map/ppermute | solution.py:15
  12.0 52.0 %collective-permute-start.11 = (bf16[128,2048]{0,1:T(8,128)(2,1)S(1)}, bf16[128,2048]{0,1:T(8,128)(2,1)S(1)}, u32[]{:S(2)}, u32[]{:S(2)}) collective-permute-start(bf16[128,2048]{0,1:T(8,128)(2,1)S(1)} %bitcast.96), channel_id=1, source_target_pairs={{0,8},{8,16},{16,24},{24,32},{32,40},{40,48},{48,56},{56,64},{64,7... | collective-permute-start | bytes 1572872 | tf_op jit(solution)/shard_map/ppermute | solution.py:15
  14.8 58.2 %collective-permute-start.10 = (bf16[128,2048]{0,1:T(8,128)(2,1)S(1)}, bf16[128,2048]{0,1:T(8,128)(2,1)S(1)}, u32[]{:S(2)}, u32[]{:S(2)}) collective-permute-start(bf16[128,2048]{0,1:T(8,128)(2,1)S(1)} %bitcast.97), channel_id=1, source_target_pairs={{0,16},{8,24},{16,32},{24,40},{32,48},{40,56},{48,64},{56,72},{64,... | collective-permute-start | bytes 1572872 | tf_op jit(solution)/shard_map/ppermute | solution.py:15
  20.0 59.0 %collective-permute-start.9 = (bf16[128,2048]{0,1:T(8,128)(2,1)S(1)}, bf16[128,2048]{0,1:T(8,128)(2,1)}, u32[]{:S(2)}, u32[]{:S(2)}) collective-permute-start(bf16[128,2048]{0,1:T(8,128)(2,1)S(1)} %bitcast.98), channel_id=1, source_target_pairs={{0,24},{8,32},{16,40},{24,48},{32,56},{40,64},{48,72},{56,80},{64,... | collective-permute-start | bytes 1572872 | tf_op jit(solution)/shard_map/ppermute | solution.py:15
  24.4 14.8 %collective-permute-start.5 = (bf16[16,128]{1,0:T(8,128)(2,1)S(1)}, bf16[16,128]{1,0:T(8,128)(2,1)S(1)}, u32[]{:S(2)}, u32[]{:S(2)}) collective-permute-start(bf16[16,128]{1,0:T(8,128)(2,1)S(1)} %fusion.14), channel_id=1, source_target_pairs={{0,24},{8,32},{16,40},{24,48},{32,56},{40,64},{48,72},{56,80},{64,... | collective-permute-start | bytes 12296 | tf_op jit(solution)/shard_map/ppermute | solution.py:15
  28.1 14.0 %collective-permute-start.4 = (bf16[16,128]{1,0:T(8,128)(2,1)S(1)}, bf16[16,128]{1,0:T(8,128)(2,1)S(1)}, u32[]{:S(2)}, u32[]{:S(2)}) collective-permute-start(bf16[16,128]{1,0:T(8,128)(2,1)S(1)} %fusion.14), channel_id=1, source_target_pairs={{0,32},{8,40},{16,48},{24,56},{32,64},{40,72},{48,80},{56,88},{64,... | collective-permute-start | bytes 12296 | tf_op jit(solution)/shard_map/ppermute | solution.py:15
  39.2 46.2 %collective-permute-start.8 = (bf16[128,2048]{0,1:T(8,128)(2,1)S(1)}, bf16[128,2048]{0,1:T(8,128)(2,1)S(1)}, u32[]{:S(2)}, u32[]{:S(2)}) collective-permute-start(bf16[128,2048]{0,1:T(8,128)(2,1)S(1)} %bitcast.100), channel_id=1, source_target_pairs={{0,32},{8,40},{16,48},{24,56},{32,64},{40,72},{48,80},{56,88},{64,... | collective-permute-start | bytes 1572872 | tf_op jit(solution)/shard_map/ppermute | solution.py:15
  42.2 55.8 %collective-permute-start.3 = (bf16[128,2048]{0,1:T(8,128)(2,1)S(1)}, bf16[128,2048]{0,1:T(8,128)(2,1)}, u32[]{:S(2)}, u32[]{:S(2)}) collective-permute-start(bf16[128,2048]{0,1:T(8,128)(2,1)S(1)} %bitcast.102), channel_id=1, source_target_pairs={{0,8},{8,16},{16,24},{24,32},{32,40},{40,48},{48,56},{56,64},{64,7... | collective-permute-start | bytes 1572872 | tf_op jit(solution)/shard_map/ppermute | solution.py:15
  64.0 36.0 %collective-permute-start.2 = (bf16[128,2048]{0,1:T(8,128)(2,1)S(1)}, bf16[128,2048]{0,1:T(8,128)(2,1)}, u32[]{:S(2)}, u32[]{:S(2)}) collective-permute-start(bf16[128,2048]{0,1:T(8,128)(2,1)S(1)} %bitcast.103), channel_id=1, source_target_pairs={{0,16},{8,24},{16,32},{24,40},{32,48},{40,56},{48,64},{56,72},{64,... | collective-permute-start | bytes 1572872 | tf_op jit(solution)/shard_map/ppermute | solution.py:15
  73.1 29.0 %collective-permute-start.1 = (bf16[128,2048]{0,1:T(8,128)(2,1)S(1)}, bf16[128,2048]{0,1:T(8,128)(2,1)}, u32[]{:S(2)}, u32[]{:S(2)}) collective-permute-start(bf16[128,2048]{0,1:T(8,128)(2,1)S(1)} %bitcast.104), channel_id=1, source_target_pairs={{0,24},{8,32},{16,40},{24,48},{32,56},{40,64},{48,72},{56,80},{64,... | collective-permute-start | bytes 1572872 | tf_op jit(solution)/shard_map/ppermute | solution.py:15
  79.0 25.1 %collective-permute-start = (bf16[128,2048]{0,1:T(8,128)(2,1)S(1)}, bf16[128,2048]{0,1:T(8,128)(2,1)}, u32[]{:S(2)}, u32[]{:S(2)}) collective-permute-start(bf16[128,2048]{0,1:T(8,128)(2,1)S(1)} %bitcast.105), channel_id=1, source_target_pairs={{0,32},{8,40},{16,48},{24,56},{32,64},{40,72},{48,80},{56,88},{64,... | collective-permute-start | bytes 1572872 | tf_op jit(solution)/shard_map/ppermute | solution.py:15
  151.9 160.1 %collective-permute-start.12 = (f32[128,2048]{0,1:T(8,128)}, f32[128,2048]{0,1:T(8,128)}, u32[]{:S(2)}, u32[]{:S(2)}) collective-permute-start(f32[128,2048]{0,1:T(8,128)} %bitcast.111), channel_id=1, source_target_pairs={{8,0},{16,8},{24,16},{32,24},{40,32},{48,40},{56,48},{64,56},{72,6... | collective-permute-start | bytes 3145736 | tf_op jit(solution)/shard_map/ppermute | solution.py:15
  182.0 132.0 %collective-permute-start.13 = (f32[128,2048]{0,1:T(8,128)}, f32[128,2048]{0,1:T(8,128)}, u32[]{:S(2)}, u32[]{:S(2)}) collective-permute-start(f32[128,2048]{0,1:T(8,128)} %bitcast.110), channel_id=1, source_target_pairs={{16,0},{24,8},{32,16},{40,24},{48,32},{56,40},{64,48},{72,56},{80,... | collective-permute-start | bytes 3145736 | tf_op jit(solution)/shard_map/ppermute | solution.py:15
  183.9 132.0 %collective-permute-start.14 = (f32[128,2048]{0,1:T(8,128)}, f32[128,2048]{0,1:T(8,128)}, u32[]{:S(2)}, u32[]{:S(2)}) collective-permute-start(f32[128,2048]{0,1:T(8,128)} %bitcast.108), channel_id=1, source_target_pairs={{24,0},{32,8},{40,16},{48,24},{56,32},{64,40},{72,48},{80,56},{88,... | collective-permute-start | bytes 3145736 | tf_op jit(solution)/shard_map/ppermute | solution.py:15
  185.8 90.0 %collective-permute-start.20 = (f32[16,128]{1,0:T(8,128)S(1)}, f32[16,128]{1,0:T(8,128)S(1)}, u32[]{:S(2)}, u32[]{:S(2)}) collective-permute-start(f32[16,128]{1,0:T(8,128)S(1)} %get-tuple-element.22), channel_id=1, source_target_pairs={{8,0},{16,8},{24,16},{32,24},{40,32},{48,40},{56,48},{64,56},{72,6... | collective-permute-start | bytes 24584 | tf_op jit(solution)/shard_map/ppermute | solution.py:15
  188.6 94.0 %collective-permute-start.23 = (f32[16,128]{1,0:T(8,128)S(1)}, f32[16,128]{1,0:T(8,128)S(1)}, u32[]{:S(2)}, u32[]{:S(2)}) collective-permute-start(f32[16,128]{1,0:T(8,128)S(1)} %get-tuple-element.23), channel_id=1, source_target_pairs={{32,0},{40,8},{48,16},{56,24},{64,32},{72,40},{80,48},{88,56},{96,... | collective-permute-start | bytes 24584 | tf_op jit(solution)/shard_map/ppermute | solution.py:15
  275.8 12.9 %collective-permute-start.22 = (f32[16,128]{1,0:T(8,128)S(1)}, f32[16,128]{1,0:T(8,128)S(1)}, u32[]{:S(2)}, u32[]{:S(2)}) collective-permute-start(f32[16,128]{1,0:T(8,128)S(1)} %get-tuple-element.24), channel_id=1, source_target_pairs={{24,0},{32,8},{40,16},{48,24},{56,32},{64,40},{72,48},{80,56},{88,... | collective-permute-start | bytes 24584 | tf_op jit(solution)/shard_map/ppermute | solution.py:15
  282.7 262.8 %collective-permute-start.15 = (f32[128,2048]{0,1:T(8,128)}, f32[128,2048]{0,1:T(8,128)}, u32[]{:S(2)}, u32[]{:S(2)}) collective-permute-start(f32[128,2048]{0,1:T(8,128)} %bitcast.109), channel_id=1, source_target_pairs={{32,0},{40,8},{48,16},{56,24},{64,32},{72,40},{80,48},{88,56},{96,... | collective-permute-start | bytes 3145736 | tf_op jit(solution)/shard_map/ppermute | solution.py:15
  288.8 15.3 %collective-permute-start.21 = (f32[16,128]{1,0:T(8,128)S(1)}, f32[16,128]{1,0:T(8,128)S(1)}, u32[]{:S(2)}, u32[]{:S(2)}) collective-permute-start(f32[16,128]{1,0:T(8,128)S(1)} %get-tuple-element.25), channel_id=1, source_target_pairs={{16,0},{24,8},{32,16},{40,24},{48,32},{56,40},{64,48},{72,56},{80,... | collective-permute-start | bytes 24584 | tf_op jit(solution)/shard_map/ppermute | solution.py:15
  304.1 244.9 %collective-permute-start.17 = (f32[128,2048]{1,0:T(8,128)}, f32[128,2048]{1,0:T(8,128)}, u32[]{:S(2)}, u32[]{:S(2)}) collective-permute-start(f32[128,2048]{1,0:T(8,128)} %copy.58), channel_id=1, source_target_pairs={{16,0},{24,8},{32,16},{40,24},{48,32},{56,40},{64,48},{72,56},{80,... | collective-permute-start | bytes 3145736 | tf_op jit(solution)/shard_map/ppermute | solution.py:15
  312.1 236.9 %collective-permute-start.18 = (f32[128,2048]{1,0:T(8,128)}, f32[128,2048]{1,0:T(8,128)}, u32[]{:S(2)}, u32[]{:S(2)}) collective-permute-start(f32[128,2048]{1,0:T(8,128)} %copy.59), channel_id=1, source_target_pairs={{24,0},{32,8},{40,16},{48,24},{56,32},{64,40},{72,48},{80,56},{88,... | collective-permute-start | bytes 3145736 | tf_op jit(solution)/shard_map/ppermute | solution.py:15
  314.0 235.0 %collective-permute-start.19 = (f32[128,2048]{1,0:T(8,128)}, f32[128,2048]{1,0:T(8,128)}, u32[]{:S(2)}, u32[]{:S(2)}) collective-permute-start(f32[128,2048]{1,0:T(8,128)} %copy.60), channel_id=1, source_target_pairs={{32,0},{40,8},{48,16},{56,24},{64,32},{72,40},{80,48},{88,56},{96,... | collective-permute-start | bytes 3145736 | tf_op jit(solution)/shard_map/ppermute | solution.py:15
  315.9 233.0 %collective-permute-start.16 = (f32[128,2048]{1,0:T(8,128)}, f32[128,2048]{1,0:T(8,128)}, u32[]{:S(2)}, u32[]{:S(2)}) collective-permute-start(f32[128,2048]{1,0:T(8,128)} %copy.56), channel_id=1, source_target_pairs={{8,0},{16,8},{24,16},{32,24},{40,32},{48,40},{56,48},{64,56},{72,6... | collective-permute-start | bytes 3145736 | tf_op jit(solution)/shard_map/ppermute | solution.py:15
  (15 other events, 267.3 us)
